TPU v7x, 128 devices: a whole 4x4x4 slice. The times are simulated.
128 devices in a mesh: band: 4 (over y_hi, core), tile: 32 (over z, x, y_lo).
Axes of the slice: x: 4, y: 4 (y_hi: 2, y_lo: 2; y = y_hi * 2 + y_lo), z: 4, core: 2. Of those that a mesh axis runs over, the one named last changes fastest.
Arguments:
- traces: float32 [256, 256, 1024], P(None, ('band', 'tile')), may hold values from -6 to 6
- bins: int32 [8], replicated, may hold values from 1 to 31, as said below
Outputs:
- dip_fields: float32 [8, 2, 256, 256, 128], P('band', None, 'tile')
Inputs may be any that keep to these rules, and one draw needn't show every extreme that they name: 8 distinct bins, 1 and 31 among them.
All inputs are finite; a program needn't handle non-finite values.
Results may differ from a plain program's by a relative error of at most 0.00018.
Values sent between devices are 32-bit elements; how exact they have to be, the bound alone decides.
A program may use at most 128 MiB of HBM per device.

v0:
```python
import math

import jax
import jax.numpy as jnp
from jax import lax
from jax.sharding import PartitionSpec as P

NT = 1024
NB = 8
WIN = 64
HOP = 8
SEG = 128
R = 3
NF = 128


smooth_sigma = 2.0
tiny_value = 1e-06


def extended_2(block, sides, width):
    for axis, dim in sides:
        count = lax.axis_size(axis)
        forward = [(i, i + 1) for i in range(count - 1)]
        backward = [(target, source) for source, target in forward]
        low = lax.ppermute(
            lax.slice_in_dim(block, block.shape[dim] - width, None, axis=dim), axis, forward
        )
        high = lax.ppermute(lax.slice_in_dim(block, 0, width, axis=dim), axis, backward)
        block = jnp.concatenate([low, block, high], axis=dim)
    return block


def window_kernel(bins):
    band_count = bins.shape[0]
    sample_index = jnp.arange(WIN, dtype=jnp.int32)
    window_taper = 0.5 - 0.5 * jnp.cos(2.0 * math.pi / WIN * sample_index.astype(jnp.float32))
    phase_turns = bins[:, None] * sample_index[None, :] % WIN
    angles = 2.0 * math.pi / WIN * phase_turns.astype(jnp.float32)
    basis_rows = jnp.stack([window_taper * jnp.cos(angles), -window_taper * jnp.sin(angles)])
    frame_count = SEG // HOP
    seg_span = SEG + WIN - HOP
    offset = (
        jnp.arange(seg_span, dtype=jnp.int32)[:, None]
        - HOP * jnp.arange(frame_count, dtype=jnp.int32)[None, :]
    )
    inside = (offset >= 0) & (offset < WIN)
    picked = jnp.take(basis_rows, jnp.clip(offset, 0, WIN - 1), axis=2)
    kernel_table = jnp.where(inside[None, None], picked, 0.0)
    return jnp.transpose(kernel_table, (2, 0, 1, 3)).reshape(seg_span, 2 * band_count * frame_count)


def band_amplitude(traces, dft_kernel):
    frame_count = SEG // HOP
    seg_span = SEG + WIN - HOP
    block_count = NT // SEG
    band_count = dft_kernel.shape[1] // (2 * frame_count)
    padded = jnp.pad(traces, ((0, 0), (0, 0), (WIN // 2, WIN // 2)))
    pieces = jnp.stack(
        [padded[:, :, block * SEG : block * SEG + seg_span] for block in range(block_count)], axis=2
    )
    spectra = jnp.dot(
        pieces, dft_kernel, precision=lax.Precision.HIGHEST, preferred_element_type=jnp.float32
    )
    spectra = spectra.reshape(
        traces.shape[0], traces.shape[1], block_count, 2, band_count, frame_count
    )
    real_part = spectra[:, :, :, 0]
    imag_part = spectra[:, :, :, 1]
    return jnp.sqrt(real_part * real_part + imag_part * imag_part)


def gradients(padded):
    grad_il = (padded[2:, 1:-1, 1:-1] - padded[:-2, 1:-1, 1:-1]) * 0.5
    grad_xl = (padded[1:-1, 2:, 1:-1] - padded[1:-1, :-2, 1:-1]) * 0.5
    grad_time = (padded[1:-1, 1:-1, 2:] - padded[1:-1, 1:-1, :-2]) * 0.5
    return (grad_il, grad_xl, grad_time)


def smooth_axis(field, axis, length):
    weights = [
        math.exp(-(offset_step * offset_step) / (2.0 * smooth_sigma * smooth_sigma))
        for offset_step in range(-R, R + 1)
    ]
    weight_sum = sum(weights)
    result = None
    for position, weight in enumerate(weights):
        section = lax.slice_in_dim(field, position, position + length, axis=axis)
        scaled = weight / weight_sum * section
        result = scaled if result is None else result + scaled
    return result


def smoothed_dips(grad_il, grad_xl, grad_time):
    width = grad_il.shape[0] - 2 * R
    stacked = jnp.stack([grad_il * grad_time, grad_xl * grad_time, grad_time * grad_time])
    along_rows = smooth_axis(stacked, 1, width)
    cross_pad = jnp.pad(along_rows, ((0, 0), (0, 0), (R, R), (0, 0)))
    along_cross = smooth_axis(cross_pad, 2, along_rows.shape[2])
    time_pad = jnp.pad(along_cross, ((0, 0), (0, 0), (0, 0), (R, R)))
    tensor = smooth_axis(time_pad, 3, along_rows.shape[3])
    denominator = tensor[2] + tiny_value
    return jnp.stack([-tensor[0] / denominator, -tensor[1] / denominator])


def local(traces, bins):
    dft_kernel = window_kernel(bins)
    amplitude = band_amplitude(traces, dft_kernel)
    n_band = lax.axis_size("band")
    n_tile = lax.axis_size("tile")
    device_count = n_band * n_tile
    il_all = traces.shape[0]
    xl_part = traces.shape[1]
    tile_rows = il_all // n_tile
    band_group = NB // n_band
    frame_count = SEG // HOP
    block_count = NT // SEG
    rim_width = R + 1
    spectrum = amplitude.reshape(il_all, xl_part, block_count, n_band, band_group, frame_count)
    by_tile = spectrum.reshape(
        n_tile, tile_rows, xl_part, block_count, n_band, band_group, frame_count
    )
    payload = jnp.transpose(by_tile, (4, 0, 5, 1, 2, 3, 6))
    payload = payload.reshape(n_band, n_tile, band_group, tile_rows, xl_part, NF)
    outgoing = payload.reshape(device_count, band_group, tile_rows, xl_part, NF)
    bricks = lax.all_to_all(outgoing, ("band", "tile"), split_axis=0, concat_axis=3, tiled=True)
    bricks = bricks.reshape(band_group, tile_rows, device_count * xl_part, NF)
    bricks = extended_2(bricks, (("tile", 1),), rim_width)
    global_row = (
        lax.axis_index("tile") * tile_rows - R + jnp.arange(tile_rows + 2 * R, dtype=jnp.int32)
    )
    inside_mask = ((global_row >= 0) & (global_row < tile_rows * n_tile)).astype(jnp.float32)[
        :, None, None
    ]

    def brick_dips(extended):
        grad_il, grad_xl, grad_time = gradients(jnp.pad(extended, ((0, 0), (1, 1), (1, 1))))
        return smoothed_dips(grad_il * inside_mask, grad_xl * inside_mask, grad_time * inside_mask)

    return lax.map(brick_dips, bricks)


def solution(mesh):
    in_specs = (P(None, ("band", "tile"), None), P())
    out_specs = P("band", None, "tile", None, None)
    return jax.shard_map(local, mesh=mesh, in_specs=in_specs, out_specs=out_specs, check_vma=False)
```

profile of v0, /device:TPU:1, one launch (start us, length us, event | category | flops | bytes accessed | tf_op | source)
XLA Modules:
  0.0 199.7 jit_solution(4386801746932931242)
XLA Ops:
  0.1 0.1 fusion.56
  0.2 2.8 %copy.52 = f32[256,2,1024]{0,2,1:T(8,128)S(1)} copy(f32[256,2,1024]{2,1,0:T(2,128)} %param.4) | data formatting | bytes 4194304 | tf_op args[0]
  3.0 0.0 copy-start.1
  3.2 0.0 copy-start
  3.2 0.4 copy-done.1
  3.7 0.1 cosine_multiply_fusion
  3.8 1.1 copy-done
  4.9 0.1 copy.62
  5.0 0.1 reshape.286
  5.1 9.6 %gather_fusion = f32[2944,2,8]{2,1,0:T(2,128)S(1)} fusion(f32[2,8,64]{1,0,2:T(2,128)S(1)} %copy.62, s32[3072]{0:T(1024)S(1)} %pad_clamp_fusion), kind=kCustom, calls=%fused_computation | custom fusion | bytes 388608 | tf_op jit(solution)/shard_map/jit(_take)/gather | solution.py:48
  14.7 3.7 %copy.72 = f32[184,16,2,8]{1,0,3,2:T(8,128)} copy(f32[184,16,2,8]{3,2,1,0:T(2,128)S(1)} %bitcast.99) | data formatting | bytes 376832 | tf_op jit(solution)/shard_map/jit(_take)/gather | solution.py:48
  18.4 0.1 copy.60
  18.5 0.1 copy.61
  18.7 1.5 select_bitcast_fusion
  20.2 0.6 copy.64
  20.8 5.9 %fusion.37 = f32[256,2,8,2,8,16]{0,5,4,3,2,1:T(8,128)S(1)} fusion(f32[256,2,8,184]{0,3,2,1:T(8,128)} %copy-done, f32[184,2,8,16]{0,3,2,1:T(8,128)S(1)} %copy.64), kind=kOutput, calls=%fused_computation.68 | convolution fusion | flops 2315255808 | bytes 7397376 | tf_op jit(solution)/shard_map/dot_general | solution.py:62
  26.6 0.7 fusion.40
  27.3 13.5 %copy.65 = f32[256,2,8,1,8,16]{5,2,4,1,0,3:T(8,128)} copy(f32[256,2,8,1,8,16]{0,5,4,3,2,1:T(8,128)S(1)} %fusion.40) | data formatting | bytes 4194304 | tf_op jit(solution)/shard_map/sqrt | solution.py:70
  40.8 16.1 %copy.66 = f32[4,32,2,8,2,8,16]{1,0,6,5,4,3,2:T(4,128)} copy(f32[4,32,2,8,2,8,16]{6,5,2,0,4,3,1:T(8,128)} %bitcast.96) | data formatting | bytes 4194304 | tf_op jit(solution)/shard_map/transpose | solution.py:123
  56.9 6.5 %reshape_reshape.4 = f32[128,2,8,2,128]{0,4,3,2,1:T(8,128)S(1)} reshape(f32[4,32,2,8,2,8,16]{1,0,6,5,4,3,2:T(4,128)} %copy.66) | data formatting | bytes 4194304 | tf_op jit(solution)/shard_map/reshape;reshape | solution.py:125
  63.4 2.3 %copy.67 = f32[128,2,8,2,128]{4,3,2,1,0:T(2,128)} copy(f32[128,2,8,2,128]{0,4,3,2,1:T(8,128)S(1)} %reshape_reshape.4) | data formatting | bytes 4194304 | tf_op jit(solution)/shard_map/reshape;reshape | solution.py:125
  65.8 42.2 %all_to_all.15 = f32[128,2,8,2,128]{4,3,2,1,0:T(2,128)S(1)} all-to-all(f32[128,2,8,2,128]{4,3,2,1,0:T(2,128)} %copy.67), channel_id=1, replica_groups=mesh['band'=4,'tile'=32] {'band','tile'}, dimensions={0} | all-to-all | bytes 4194304 | tf_op jit(solution)/shard_map/all_to_all | solution.py:126
  107.9 0.2 copy.68
  108.1 1.3 fusion.66
  109.4 2.3 %collective-permute-start = (f32[2,4,256,128]{3,1,2,0:T(4,128)}, f32[2,4,256,128]{3,1,2,0:T(4,128)}, u32[]{:S(2)}, u32[]{:S(2)}) collective-permute-start(f32[2,4,256,128]{3,1,2,0:T(4,128)} %get-tuple-element.97), channel_id=1, source_target_pairs={{0,1},{1,2},{2,3},{3,4},{4,5},{5,6},{6,7},{7,8},{8,9},{9,10},{10,1... | collective-permute-start | bytes 3145736 | tf_op jit(solution)/shard_map/ppermute | solution.py:26
  111.7 1.5 collective-permute-start.1
  113.2 41.4 %collective-permute-done = f32[2,4,256,128]{3,1,2,0:T(4,128)} collective-permute-done((f32[2,4,256,128]{3,1,2,0:T(4,128)}, f32[2,4,256,128]{3,1,2,0:T(4,128)}, u32[]{:S(2)}, u32[]{:S(2)}) %collective-permute-start) | collective-permute-done | bytes 1048608 | tf_op jit(solution)/shard_map/ppermute | solution.py:26
  154.6 5.7 %collective-permute-done.1 = f32[2,4,256,128]{3,1,2,0:T(4,128)} collective-permute-done((f32[2,4,256,128]{3,1,2,0:T(4,128)S(1)}, f32[2,4,256,128]{3,1,2,0:T(4,128)}, u32[]{:S(2)}, u32[]{:S(2)}) %collective-permute-start.1) | collective-permute-done | bytes 1048608 | tf_op jit(solution)/shard_map/ppermute | solution.py:29
  160.3 4.2 %pad_maximum_fusion.1 = f32[2,16,256,128]{3,1,2,0:T(8,128)} fusion(f32[2,4,256,128]{3,1,2,0:T(4,128)} %collective-permute-done.1, f32[2,8,256,128]{3,1,2,0:T(8,128)S(1)} %bitcast.98, f32[2,4,256,128]{3,1,2,0:T(4,128)} %collective-permute-done), kind=kLoop, calls=%fused_computation.67 | loop fusion | flops 2097152 | bytes 8388608 | tf_op jit(solution)/shard_map/concatenate | solution.py:30
  164.6 35.2 %while.13 = (s32[]{:T(128)}, f32[2,2,8,256,128]{4,3,2,1,0:T(8,128)}, f32[2,16,256,128]{3,1,2,0:T(8,128)}, s32[]{:T(128)}, s32[]{:T(128)}) while((s32[]{:T(128)}, f32[2,2,8,256,128]{4,3,2,1,0:T(8,128)}, f32[2,16,256,128]{3,1,2,0:T(8,128)}, s32[]{:T(128)}, s32[]{:T(128)}) %tuple.46), condition=%wide.region_1.2_spmd.clone, body=%wide.region_0.1_spmd.clone.sunk | while | flops 41222216 | bytes 77857456 | solution.py:140
  164.6 1.7 constant_dynamic-slice_fusion.2
  166.3 0.7 copy.78
  167.0 3.1 %fusion.74 = (f32[1,14,256,128]{3,2,1,0:T(8,128)S(1)}, f32[1,14,256,128]{3,2,1,0:T(8,128)S(1)}, f32[1,14,256,128]{3,2,1,0:T(8,128)S(1)}) fusion(f32[1,16,256,128]{3,2,1,0:T(8,128)S(1)} %copy.78, f32[14]{0:T(128)S(1)} %fusion.73, f32[16,256,128]{2,1,0:T(8,128)S(1)} %bitcast.95), kind=kLoop, calls=%fused_computation.56.clone.1 | loop fusion | flops 5963776 | bytes 11272248 | tf_op jit(solution)/shard_map/while/body/eval_jaxpr/stack | solution.py:96
  170.1 0.6 pad_maximum_fusion.4
  170.7 2.1 %fusion.75 = f32[3,8,256,128]{3,2,1,0:T(8,128)S(1)} fusion(f32[3,14,256,128]{3,2,1,0:T(8,128)S(1)} %pad_maximum_fusion.4), kind=kLoop, calls=%fused_computation.26.clone.1 | loop fusion | flops 10223616 | bytes 25165824 | tf_op jit(solution)/shard_map/while/body/eval_jaxpr/add | solution.py:90
  172.8 2.6 %multiply_add_fusion.2 = f32[3,8,256,128]{3,2,1,0:T(8,128)S(1)} fusion(f32[3,8,256,128]{3,2,1,0:T(8,128)S(1)} %fusion.75), kind=kLoop, calls=%fused_computation.38.clone.1 | loop fusion | flops 10223616 | bytes 6291456 | tf_op jit(solution)/shard_map/while/body/eval_jaxpr/add | solution.py:90
  175.4 5.0 %fusion.76 = f32[3,8,256,128]{3,2,1,0:T(8,128)S(1)} fusion(f32[3,8,256,128]{3,2,1,0:T(8,128)S(1)} %multiply_add_fusion.2), kind=kLoop, calls=%fused_computation.19.clone.1 | loop fusion | flops 10223616 | bytes 6291456 | tf_op jit(solution)/shard_map/while/body/eval_jaxpr/add | solution.py:90
  180.4 0.3 fusion.77
  180.7 1.5 fusion.78
  182.1 1.7 constant_dynamic-slice_fusion.2
  183.9 0.7 copy.78
  184.6 3.1 %fusion.74 = (f32[1,14,256,128]{3,2,1,0:T(8,128)S(1)}, f32[1,14,256,128]{3,2,1,0:T(8,128)S(1)}, f32[1,14,256,128]{3,2,1,0:T(8,128)S(1)}) fusion(f32[1,16,256,128]{3,2,1,0:T(8,128)S(1)} %copy.78, f32[14]{0:T(128)S(1)} %fusion.73, f32[16,256,128]{2,1,0:T(8,128)S(1)} %bitcast.95), kind=kLoop, calls=%fused_computation.56.clone.1 | loop fusion | flops 5963776 | bytes 11272248 | tf_op jit(solution)/shard_map/while/body/eval_jaxpr/stack | solution.py:96
  187.7 0.6 pad_maximum_fusion.4
  188.3 2.1 %fusion.75 = f32[3,8,256,128]{3,2,1,0:T(8,128)S(1)} fusion(f32[3,14,256,128]{3,2,1,0:T(8,128)S(1)} %pad_maximum_fusion.4), kind=kLoop, calls=%fused_computation.26.clone.1 | loop fusion | flops 10223616 | bytes 25165824 | tf_op jit(solution)/shard_map/while/body/eval_jaxpr/add | solution.py:90
  190.3 2.6 %multiply_add_fusion.2 = f32[3,8,256,128]{3,2,1,0:T(8,128)S(1)} fusion(f32[3,8,256,128]{3,2,1,0:T(8,128)S(1)} %fusion.75), kind=kLoop, calls=%fused_computation.38.clone.1 | loop fusion | flops 10223616 | bytes 6291456 | tf_op jit(solution)/shard_map/while/body/eval_jaxpr/add | solution.py:90
  192.9 5.0 %fusion.76 = f32[3,8,256,128]{3,2,1,0:T(8,128)S(1)} fusion(f32[3,8,256,128]{3,2,1,0:T(8,128)S(1)} %multiply_add_fusion.2), kind=kLoop, calls=%fused_computation.19.clone.1 | loop fusion | flops 10223616 | bytes 6291456 | tf_op jit(solution)/shard_map/while/body/eval_jaxpr/add | solution.py:90
  198.0 0.3 fusion.77
  198.2 1.5 fusion.78
  (16 shorter events, 0.3 us)
Async XLA Ops:
  3.0 0.7 copy-start.1
  3.2 1.6 copy-start
  109.4 45.2 %collective-permute-start = (f32[2,4,256,128]{3,1,2,0:T(4,128)}, f32[2,4,256,128]{3,1,2,0:T(4,128)}, u32[]{:S(2)}, u32[]{:S(2)}) collective-permute-start(f32[2,4,256,128]{3,1,2,0:T(4,128)} %get-tuple-element.97), channel_id=1, source_target_pairs={{0,1},{1,2},{2,3},{3,4},{4,5},{5,6},{6,7},{7,8},{8,9},{9,10},{10,1... | collective-permute-start | bytes 3145736 | tf_op jit(solution)/shard_map/ppermute | solution.py:26
  111.7 48.7 %collective-permute-start.1 = (f32[2,4,256,128]{3,1,2,0:T(4,128)S(1)}, f32[2,4,256,128]{3,1,2,0:T(4,128)}, u32[]{:S(2)}, u32[]{:S(2)}) collective-permute-start(f32[2,4,256,128]{3,1,2,0:T(4,128)S(1)} %get-tuple-element.98), channel_id=1, source_target_pairs={{1,0},{2,1},{3,2},{4,3},{5,4},{6,5},{7,6},{8,7},{9,8},{10,9},{11,1... | collective-permute-start | bytes 3145736 | tf_op jit(solution)/shard_map/ppermute | solution.py:29
where the time goes:
time: 200 us
  local copies, waits for them, and re-layouts  63.5 us (32%)
  waiting for transfers between devices  47.2 us (24%)
  blocking collectives  42.2 us (21%)
  other arithmetic  36.9 us (18%)
  matrix products  5.88 us (3%)
  starting transfers between devices  3.75 us (2%)
    all_to_all x1, blocking collectives, local(): lax.all_to_all(outgoing, ('band', 'tile'), split_axis=0, concat_axis=3, t...  42.2 us
    ppermute x1, waiting for transfers between devices, extended_2(): lax.ppermute(lax.slice_in_dim(block, block.shape[dim] - width, None, axis...  41.4 us
    add x6, other arithmetic, smooth_axis(): result = scaled if result is None else result + scaled  19.4 us
    transpose x1, local copies, waits for them, and re-layouts, local(): payload = jnp.transpose(by_tile, (4, 0, 5, 1, 2, 3, 6))  16.1 us
    sqrt x1, local copies, waits for them, and re-layouts, band_amplitude(): return jnp.sqrt(real_part * real_part + imag_part * imag_part)  13.5 us
    gather x2, local copies, waits for them, and re-layouts, window_kernel(): picked = jnp.take(basis_rows, jnp.clip(offset, 0, WIN - 1), axis=2)  13.3 us
    another operation x2, local copies, waits for them, and re-layouts, local(): outgoing = payload.reshape(device_count, band_group, tile_rows, xl_part, NF)  8.86 us
    another operation x4, other arithmetic, smoothed_dips(): jnp.stack([grad_il * grad_time, grad_xl * grad_time, grad_time * grad_time])  7.36 us
  transfers between devices with their start and end apart: 2, of which 2 were waited for; matrix products, arithmetic and copies ran while one was open for 0% of the time, Pallas kernels for 0%

commit v1 on v0

v1 whole, which is shorter than its diff:
```python
import functools
import math

import jax
import jax.numpy as jnp
import numpy as np
from jax import lax
from jax.experimental import pallas as pl
from jax.experimental.pallas import tpu as pltpu
from jax.sharding import PartitionSpec as P

WIN = 64
R = 3
NF = 128
SIGMA = 2.0
TINY = 1e-6
MESH = pl.DeviceIdType.MESH
LANES = 128
ROWS = 288
CH = 32
GX = 32


def smooth_weights():
    w = [math.exp(-(k * k) / (2.0 * SIGMA * SIGMA)) for k in range(-R, R + 1)]
    total = sum(w)
    return [v / total for v in w]


def time_matrix():
    w = smooth_weights()
    m = np.zeros((NF, NF), np.float64)
    for lane in range(NF):
        f = (lane + 4) % NF
        for k in range(-R, R + 1):
            if 0 <= f + k < NF:
                m[lane, f + k] = w[k + R]
    hi = m.astype(jnp.bfloat16)
    lo = (m - hi.astype(np.float64)).astype(jnp.bfloat16)
    zero = np.zeros_like(lo)
    return np.concatenate(
        [np.concatenate([hi, lo], axis=1), np.concatenate([hi, zero], axis=1)], axis=0
    )


def split(x):
    hi = x.astype(jnp.bfloat16)
    return hi, (x - hi.astype(jnp.float32)).astype(jnp.bfloat16)


def build_table(bins_ref, wh, wl):
    k = lax.broadcasted_iota(jnp.int32, (256, LANES), 0)
    lane = lax.broadcasted_iota(jnp.int32, (256, LANES), 1)
    group = lane // 16
    bins = jnp.zeros((256, LANES), jnp.int32)
    for b in range(8):
        bins = jnp.where(group == b, bins_ref[b], bins)
    frame = lane % 16
    n = k - 8 * frame
    inside = (n >= 0) & (n < WIN)
    step = 2.0 * math.pi / WIN
    taper = 0.5 - 0.5 * jnp.cos(step * n.astype(jnp.float32))
    angle = step * ((bins * n) & (WIN - 1)).astype(jnp.float32)
    re = jnp.where(inside, taper * jnp.cos(angle), 0.0)
    im = jnp.where(inside, -(taper * jnp.sin(angle)), 0.0)
    keep = (frame < 12) == (k < 128)
    for c, part in enumerate((re, im)):
        cols = slice(c * LANES, (c + 1) * LANES)
        for s, value in enumerate((part, jnp.where(keep, part, 0.0))):
            hi, lo = split(value)
            wh[s, :, cols] = hi
            wl[s, :, cols] = lo


def amplitude_step(c, xv, wh, wl, send):
    group = lax.broadcasted_iota(jnp.int32, (CH, LANES), 1) // 16
    for e in range(2):
        tiles = [
            split(xv[pl.ds(c * (CH * 16) + 2 * t + e, CH, stride=16), :]) for t in range(8)
        ]
        wide = [
            [jnp.concatenate([tiles[s][h], tiles[(s + 1) % 8][h]], axis=1) for s in range(8)]
            for h in range(2)
        ]

        def product(first, last, table):
            hi = jnp.concatenate(wide[0][first:last], axis=0)
            lo = jnp.concatenate(wide[1][first:last], axis=0)
            dot = functools.partial(jnp.dot, preferred_element_type=jnp.float32)
            return dot(hi, wh[table]) + dot(lo, wh[table]) + dot(hi, wl[table])

        spec = jnp.concatenate([product(0, 7, 0), product(7, 8, 1)], axis=0)
        re, im = spec[:, :LANES], spec[:, LANES:]
        amp = jnp.sqrt(re * re + im * im)
        v = [amp[s * CH : (s + 1) * CH] for s in range(8)]
        for d in (4, 2, 1):
            low = (group & d) == 0
            for i in range(8):
                if i & d == 0:
                    a, b = v[i], v[i + d]
                    v[i] = jnp.where(low, a, pltpu.roll(b, 16 * d, axis=1))
                    v[i + d] = jnp.where(low, pltpu.roll(a, LANES - 16 * d, axis=1), b)
        for b in range(8):
            send[b, e, pl.ds(pl.multiple_of(c * CH, CH), CH), :] = v[b]


def products_step(g, recv, q):
    lane = lax.broadcasted_iota(jnp.int32, (8, LANES), 1)
    w = smooth_weights()

    def rows(xl, row):
        return recv[pl.ds((8 * g + xl + 1) * 16 + row, 8, stride=16), :]

    a = [rows(0, r) for r in range(16)]
    p = [[], [], []]
    for r in range(1, 15):
        later = jnp.where(lane == 123, 0.0, pltpu.roll(a[r], LANES - 1, axis=1))
        earlier = jnp.where(lane == 124, 0.0, pltpu.roll(a[r], 1, axis=1))
        gt = later - earlier
        p[0].append((a[r + 1] - a[r - 1]) * gt)
        p[1].append((rows(1, r) - rows(-1, r)) * gt)
        p[2].append(gt * gt)
    for i in range(3):
        for r in range(8):
            s = w[3] * p[i][r + 3]
            for k in range(1, 4):
                s = s + w[3 + k] * (p[i][r + 3 - k] + p[i][r + 3 + k])
            q[i, pl.ds((8 * g + 3) * 8 + r, 8, stride=8), :] = s


def smooth_step(g, q, tmat, out):
    w = smooth_weights()
    sm = []
    for i in range(3):
        load = lambda x: q[i, pl.ds(pl.multiple_of((GX * g + x) * 8, 8), GX * 8), :]
        s = w[3] * load(3)
        for k in range(1, 4):
            s = s + w[3 + k] * (load(3 - k) + load(3 + k))
        sm.append(s)
    hi, lo = split(jnp.concatenate(sm, axis=0))
    t = jnp.dot(
        jnp.concatenate([hi, lo], axis=1), tmat[...], preferred_element_type=jnp.float32
    )
    t = t[:, :LANES] + t[:, LANES:]
    m = GX * 8
    inv = -1.0 / (t[2 * m :] + 4.0 * TINY)
    for i in range(2):
        d = t[i * m : (i + 1) * m] * inv
        for x in range(GX):
            out[i, pl.ds(GX * g + x, 8, stride=256), :] = d[8 * x : 8 * x + 8]


def kernel(
    x_hbm, bins_ref, tmat, out_hbm, xv, wh, wl, send, recv, q, out, in_sem, ssem, rsem, own_sem, osem
):
    band, tile = lax.axis_index("band"), lax.axis_index("tile")
    me = band * 32 + tile
    z, x = tile // 8, (tile // 2) % 4
    y, core = (band // 2) * 2 + tile % 2, band % 2

    def partner(k):
        k = lax.rem(k * 85, 128)
        dc, dz, dx, dy = k // 64, (k // 16) % 4, (k // 4) % 4, k % 4
        z2, x2, y2, c2 = (z + dz) % 4, (x + dx) % 4, (y + dy) % 4, (core + dc) % 2
        return (y2 // 2) * 2 + c2, z2 * 8 + x2 * 2 + y2 % 2

    barrier = pltpu.get_barrier_semaphore()

    def greet(k, carry):
        pl.semaphore_signal(barrier, inc=1, device_id=partner(k), device_id_type=MESH)
        return carry

    load = pltpu.make_async_copy(x_hbm, xv.at[pl.ds(64, 4096)], in_sem)
    load.start()
    lax.fori_loop(1, 128, greet, 0)
    build_table(bins_ref, wh, wl)
    xv[pl.ds(0, 64), :] = jnp.zeros((64, LANES), jnp.float32)
    xv[pl.ds(4160, 16 * ROWS - 4160), :] = jnp.zeros((16 * ROWS - 4160, LANES), jnp.float32)
    for j in range(2):
        recv[j, pl.ds(0, 16), :] = jnp.zeros((16, LANES), jnp.float32)
        recv[j, pl.ds(257 * 16, 16), :] = jnp.zeros((16, LANES), jnp.float32)
    for i in range(3):
        q[i, pl.ds(0, 24), :] = jnp.zeros((24, LANES), jnp.float32)
        q[i, pl.ds(259 * 8, 24), :] = jnp.zeros((24, LANES), jnp.float32)
    load.wait()

    def amp(c, carry):
        amplitude_step(c, xv, wh, wl, send)
        return carry

    lax.fori_loop(0, ROWS // CH, amp, 0)
    pl.semaphore_wait(barrier, 127)

    def chunk(j, e, b2, t2):
        return (
            send.at[b2 * 2 + j, e, pl.ds(pl.multiple_of(t2 * 8, 8), 16)],
            recv.at[j, pl.ds(pl.multiple_of((2 * me + e + 1) * 16, 16), 16)],
        )

    def push(j):
        def body(k, carry):
            b2, t2 = partner(k)
            for e in range(2):
                src, dst = chunk(j, e, b2, t2)
                pltpu.make_async_remote_copy(
                    src, dst, ssem, rsem.at[j], device_id=(b2, t2), device_id_type=MESH
                ).start()
            return carry

        lax.fori_loop(1, 128, body, 0)
        own = []
        for e in range(2):
            src, dst = chunk(j, e, band, tile)
            own.append(pltpu.make_async_copy(src, dst, own_sem.at[j, e]))
            own[-1].start()
        return own

    own = [push(0), push(1)]

    def arrivals(j):
        part = pl.ds(16, 254 * 16)
        return pltpu.make_async_remote_copy(
            recv.at[j, part],
            recv.at[j, part],
            ssem,
            rsem.at[j],
            device_id=(band, lax.rem(tile + 1, 32)),
            device_id_type=MESH,
        )

    results = []
    for j in range(2):
        for copy in own[j]:
            copy.wait()
        arrivals(j).wait_recv()

        def prod(g, carry):
            products_step(g, recv.at[j], q)
            return carry

        def smooth(g, carry):
            smooth_step(g, q, tmat, out.at[j])
            return carry

        lax.fori_loop(0, 32, prod, 0)
        lax.fori_loop(0, 256 // GX, smooth, 0)
        results.append(pltpu.make_async_copy(out.at[j], out_hbm.at[j], osem.at[j]))
        results[-1].start()
    for j in range(2):
        arrivals(j).wait_send()
    for copy in results:
        copy.wait()


def local(traces, bins):
    x = traces.reshape(256, 2, 8, LANES).transpose(0, 2, 1, 3).reshape(4096, LANES)
    tmat = jnp.asarray(time_matrix())
    f32 = jnp.float32
    out = pl.pallas_call(
        kernel,
        out_shape=jax.ShapeDtypeStruct((2, 2, 2048, LANES), f32),
        in_specs=[
            pl.BlockSpec(memory_space=pl.ANY),
            pl.BlockSpec(memory_space=pltpu.SMEM),
            pl.BlockSpec(memory_space=pltpu.VMEM),
        ],
        out_specs=pl.BlockSpec(memory_space=pl.ANY),
        scratch_shapes=[
            pltpu.VMEM((16 * ROWS, LANES), f32),
            pltpu.VMEM((2, 256, 256), jnp.bfloat16),
            pltpu.VMEM((2, 256, 256), jnp.bfloat16),
            pltpu.VMEM((8, 2, ROWS, LANES), f32),
            pltpu.VMEM((2, 258 * 16, LANES), f32),
            pltpu.VMEM((3, 262 * 8, LANES), f32),
            pltpu.VMEM((2, 2, 2048, LANES), f32),
            pltpu.SemaphoreType.DMA,
            pltpu.SemaphoreType.DMA,
            pltpu.SemaphoreType.DMA((2,)),
            pltpu.SemaphoreType.DMA((2, 2)),
            pltpu.SemaphoreType.DMA((2,)),
        ],
        compiler_params=pltpu.CompilerParams(
            collective_id=0, has_side_effects=True, vmem_limit_bytes=60 << 20
        ),
        name="spectral_dips",
    )(x, bins, tmat)
    return out.reshape(2, 2, 8, 256, NF)


def solution(mesh):
    in_specs = (P(None, ("band", "tile"), None), P())
    out_specs = P("band", None, "tile", None, None)
    return jax.shard_map(local, mesh=mesh, in_specs=in_specs, out_specs=out_specs, check_vma=False)
```

time: 200 us -> 84.9 us (0.42)
  the two profiles are of different devices: /device:TPU:1 before, /device:TPU:57 now
where the time goes in v1:
time: 84.9 us; the launch traced here: 84.8 us
  Pallas kernels  80.1 us (94%)
  local copies, waits for them, and re-layouts  4.65 us (5%)
    pallas_call x1, Pallas kernels, local(): pl.pallas_call(kernel, out_shape=jax.ShapeDtypeStruct((2, 2, 2048, LANES)...  80.1 us
    unnamed x1, local copies, waits for them, and re-layouts  4.65 us

profile of v1, /device:TPU:57, one launch (start us, length us, event | category | flops | bytes accessed | tf_op | source)
XLA Modules:
  0.0 84.8 jit_solution(10006297015772617900)
XLA Ops:
  0.0 80.1 %spectral_dips.1 = f32[2,2,2048,128]{3,2,1,0:T(8,128)} custom-call(f32[4096,128]{1,0:T(8,128)} %bitcast.7, s32[8]{0:T(128)} %bins_ref.1, bf16[256,256]{1,0:T(8,128)(2,1)} %constant.2.clone.tmat), custom_call_target="tpu_custom_call" | custom-call | tf_op jit(solution)/shard_map/spectral_dips/pallas_call | solution.py:259
  80.1 4.7 %copy.6 = f32[2,2,8,256,128]{4,3,2,1,0:T(8,128)} copy(f32[2,2,8,256,128]{4,3,2,1,0:T(8,128)} %bitcast.6) | data formatting | bytes 8388608

commit v2 on v1

v2 whole, which is shorter than its diff:
```python
import functools
import math

import jax
import jax.numpy as jnp
from jax import lax
from jax.experimental import pallas as pl
from jax.experimental.pallas import tpu as pltpu
from jax.sharding import PartitionSpec as P

WIN = 64
R = 3
NF = 128
SIGMA = 2.0
TINY = 1e-6
MESH = pl.DeviceIdType.MESH
LANES = 128
TILES = 4
CH = 8 * TILES + 8
GX = 32


def smooth_weights():
    w = [math.exp(-(k * k) / (2.0 * SIGMA * SIGMA)) for k in range(-R, R + 1)]
    total = sum(w)
    return [v / total for v in w]


def split(x):
    hi = x.astype(jnp.bfloat16)
    return hi, (x - hi.astype(jnp.float32)).astype(jnp.bfloat16)


def build_time_matrix(tmat):
    lane = lax.broadcasted_iota(jnp.int32, (NF, NF), 0)
    frame = lax.broadcasted_iota(jnp.int32, (NF, NF), 1)
    away = jnp.abs(((lane + 4) & (NF - 1)) - frame)
    value = jnp.zeros((NF, NF), jnp.float32)
    for k, weight in enumerate(smooth_weights()[R:]):
        value = jnp.where(away == k, weight, value)
    hi, lo = split(value)
    tmat[pl.ds(0, NF), pl.ds(0, NF)] = hi
    tmat[pl.ds(NF, NF), pl.ds(0, NF)] = hi
    tmat[pl.ds(0, NF), pl.ds(NF, NF)] = lo
    tmat[pl.ds(NF, NF), pl.ds(NF, NF)] = jnp.zeros((NF, NF), jnp.bfloat16)


def build_table(bins_ref, wh, wl):
    k = lax.broadcasted_iota(jnp.int32, (256, LANES), 0)
    lane = lax.broadcasted_iota(jnp.int32, (256, LANES), 1)
    group = lane // 16
    bins = jnp.zeros((256, LANES), jnp.int32)
    for b in range(8):
        bins = jnp.where(group == b, bins_ref[b], bins)
    frame = lane % 16
    n = k - 8 * frame
    inside = (n >= 0) & (n < WIN)
    step = 2.0 * math.pi / WIN
    taper = 0.5 - 0.5 * jnp.cos(step * n.astype(jnp.float32))
    angle = step * ((bins * n) & (WIN - 1)).astype(jnp.float32)
    re = jnp.where(inside, taper * jnp.cos(angle), 0.0)
    im = jnp.where(inside, -(taper * jnp.sin(angle)), 0.0)
    keep = (frame < 12) == (k < 128)
    for c, part in enumerate((re, im)):
        cols = slice(c * LANES, (c + 1) * LANES)
        for s, value in enumerate((part, jnp.where(keep, part, 0.0))):
            hi, lo = split(value)
            wh[s, :, cols] = hi
            wl[s, :, cols] = lo


def amplitude_step(c, xv, wh, wl, send):
    group = lax.broadcasted_iota(jnp.int32, (CH, LANES), 1) // 16
    tiles = [
        [xv[pl.ds(c * (TILES * 128) + 2 * t + e, CH, stride=16), :] for t in range(8)]
        for e in range(2)
    ]

    def product(segments, table):
        hi, lo = split(
            jnp.concatenate(
                [
                    jnp.concatenate([tiles[e][s], tiles[e][(s + 1) % 8]], axis=1)
                    for e in range(2)
                    for s in segments
                ],
                axis=0,
            )
        )
        dot = functools.partial(jnp.dot, preferred_element_type=jnp.float32)
        spec = dot(hi, wh[table]) + dot(lo, wh[table]) + dot(hi, wl[table])
        re, im = spec[:, :LANES], spec[:, LANES:]
        amp = jnp.sqrt(re * re + im * im)
        n = len(segments)
        return [
            [amp[(e * n + s) * CH : (e * n + s + 1) * CH] for s in range(n)] for e in range(2)
        ]

    first, last = product(range(7), 0), product([7], 1)
    for e in range(2):
        v = first[e] + last[e]
        for d in (4, 2, 1):
            low = (group & d) == 0
            for i in range(8):
                if i & d == 0:
                    a, b = v[i], v[i + d]
                    v[i] = jnp.where(low, a, pltpu.roll(b, 16 * d, axis=1))
                    v[i + d] = jnp.where(low, pltpu.roll(a, LANES - 16 * d, axis=1), b)
        for b in range(8):
            send[c, b, e] = v[b]


def products_step(g, recv, q):
    lane = lax.broadcasted_iota(jnp.int32, (8, LANES), 1)
    w = smooth_weights()

    def rows(xl, row):
        return recv[pl.ds((8 * g + xl + 1) * 16 + row, 8, stride=16), :]

    a = [rows(0, r) for r in range(16)]
    p = [[], [], []]
    for r in range(1, 15):
        later = jnp.where(lane == 123, 0.0, pltpu.roll(a[r], LANES - 1, axis=1))
        earlier = jnp.where(lane == 124, 0.0, pltpu.roll(a[r], 1, axis=1))
        gt = later - earlier
        p[0].append((a[r + 1] - a[r - 1]) * gt)
        p[1].append((rows(1, r) - rows(-1, r)) * gt)
        p[2].append(gt * gt)
    for i in range(3):
        for r in range(8):
            s = w[3] * p[i][r + 3]
            for k in range(1, 4):
                s = s + w[3 + k] * (p[i][r + 3 - k] + p[i][r + 3 + k])
            q[i, pl.ds((8 * g + 3) * 8 + r, 8, stride=8), :] = s


def smooth_step(g, q, tmat, out):
    w = smooth_weights()
    sm = []
    for i in range(3):
        load = lambda x: q[i, pl.ds(pl.multiple_of((GX * g + x) * 8, 8), GX * 8), :]
        s = w[3] * load(3)
        for k in range(1, 4):
            s = s + w[3 + k] * (load(3 - k) + load(3 + k))
        sm.append(s)
    hi, lo = split(jnp.concatenate(sm, axis=0))
    t = jnp.dot(
        jnp.concatenate([hi, lo], axis=1), tmat[...], preferred_element_type=jnp.float32
    )
    t = t[:, :LANES] + t[:, LANES:]
    m = GX * 8
    inv = -1.0 / (t[2 * m :] + 4.0 * TINY)
    for i in range(2):
        d = t[i * m : (i + 1) * m] * inv
        for x in range(GX):
            out[i, pl.ds(GX * g + x, 8, stride=256), :] = d[8 * x : 8 * x + 8]


def exchange_kernel(
    x_hbm, bins_hbm, dip, last, xv, bins_ref, wh, wl, send, recv, q, tmat, in_sem, ssem, rsem, own_sem
):
    band, tile = lax.axis_index("band"), lax.axis_index("tile")
    me = band * 32 + tile
    home = tile >> 2

    def partner(k):
        other = me ^ k
        return other >> 5, other & 31

    barrier = pltpu.get_barrier_semaphore()

    def greet(k, carry):
        pl.semaphore_signal(barrier, inc=1, device_id=partner(k), device_id_type=MESH)
        return carry

    load = pltpu.make_async_copy(x_hbm, xv.at[pl.ds(64, 4096)], in_sem.at[0])
    load.start()
    load_bins = pltpu.make_async_copy(bins_hbm, bins_ref, in_sem.at[1])
    load_bins.start()
    lax.fori_loop(1, 128, greet, 0)
    load_bins.wait()
    build_table(bins_ref, wh, wl)
    build_time_matrix(tmat)
    for start in (0, 4160):
        xv[pl.ds(start, 64), :] = jnp.zeros((64, LANES), jnp.float32)
    for start in (0, 257 * 16):
        recv[pl.ds(start, 16), :] = jnp.zeros((16, LANES), jnp.float32)
        last[pl.ds(start, 16), :] = jnp.zeros((16, LANES), jnp.float32)
    clear_rim(q)
    load.wait()

    def step_of(half, m):
        return (m << 1) | ((m ^ (m >> 1) ^ half) & 1)

    def form(half):
        def body(m, carry):
            amplitude_step(home ^ step_of(half, m), xv, wh, wl, send)
            return carry

        lax.fori_loop(0, 4, body, 0)

    def chunk(j, e, b2, t2):
        source = send.at[t2 >> 2, b2 * 2 + j, e, pl.ds(pl.multiple_of((t2 & 3) * 8, 8), 16)]
        place = pl.ds(pl.multiple_of((2 * me + e + 1) * 16, 16), 16)
        return source, (recv, last)[j].at[place]

    def push(j, k):
        b2, t2 = partner(k)
        for e in range(2):
            src, dst = chunk(j, e, b2, t2)
            pltpu.make_async_remote_copy(
                src, dst, ssem.at[j], rsem.at[j], device_id=(b2, t2), device_id_type=MESH
            ).start()

    def push_half(half):
        def body(n, carry):
            n = (n * 5) & 63
            push(0, ((n & 48) << 1) | (step_of(half, (n >> 2) & 3) << 2) | (n & 3))
            return carry

        lax.fori_loop(1 - half, 64, body, 0)

    def keep(j):
        own = []
        for e in range(2):
            src, dst = chunk(j, e, band, tile)
            own.append(pltpu.make_async_copy(src, dst, own_sem.at[j, e]))
            own[-1].start()
        return own

    form(0)
    pl.semaphore_wait(barrier, 127)
    own = keep(0)
    push_half(0)
    form(1)
    push_half(1)

    def arrivals(j):
        part = (recv, last)[j].at[pl.ds(16, 254 * 16)]
        return pltpu.make_async_remote_copy(
            part,
            part,
            ssem.at[j],
            rsem.at[j],
            device_id=(band, tile ^ 1),
            device_id_type=MESH,
        )

    def second(k, carry):
        push(1, (k * 75) & 127)
        return carry

    lax.fori_loop(1, 128, second, 0)
    own += keep(1)
    for copy in own[:2]:
        copy.wait()
    arrivals(0).wait_recv()

    def prod(g, carry):
        products_step(g, recv, q)
        return carry

    def smooth(g, carry):
        smooth_step(g, q, tmat, dip)
        return carry

    lax.fori_loop(0, 32, prod, 0)
    lax.fori_loop(0, 256 // GX, smooth, 0)
    for copy in own[2:]:
        copy.wait()
    arrivals(1).wait_recv()
    for j in range(2):
        arrivals(j).wait_send()


def clear_rim(q):
    for i in range(3):
        for start in (0, 259 * 8):
            q[i, pl.ds(start, 24), :] = jnp.zeros((24, LANES), jnp.float32)


def dips_kernel(dip, last, out_hbm, q, out, tmat, sems):
    give = pltpu.make_async_copy(dip, out_hbm.at[0], sems.at[0])
    give.start()
    clear_rim(q)
    build_time_matrix(tmat)

    def prod(g, carry):
        products_step(g, last, q)
        return carry

    def smooth(g, carry):
        smooth_step(g, q, tmat, out)
        return carry

    lax.fori_loop(0, 32, prod, 0)
    lax.fori_loop(0, 256 // GX, smooth, 0)
    result = pltpu.make_async_copy(out, out_hbm.at[1], sems.at[1])
    result.start()
    result.wait()
    give.wait()


def local(traces, bins):
    x = traces.reshape(256, 2, 8, LANES).transpose(0, 2, 1, 3).reshape(4096, LANES)
    x = pltpu.with_memory_space_constraint(x, pltpu.HBM)
    bins = pltpu.with_memory_space_constraint(bins, pltpu.HBM)
    f32 = jnp.float32
    dma = pltpu.SemaphoreType.DMA
    anywhere = pl.BlockSpec(memory_space=pl.ANY)
    in_vmem = pl.BlockSpec(memory_space=pltpu.VMEM)
    field = pltpu.VMEM((2, 2048, LANES), f32)
    window = pltpu.VMEM((258 * 16, LANES), f32)
    tensor = pltpu.VMEM((3, 262 * 8, LANES), f32)
    matrix = pltpu.VMEM((2 * NF, 2 * NF), jnp.bfloat16)
    dip, last = pl.pallas_call(
        exchange_kernel,
        out_shape=(
            jax.ShapeDtypeStruct((2, 2048, LANES), f32),
            jax.ShapeDtypeStruct((258 * 16, LANES), f32),
        ),
        in_specs=[pl.BlockSpec(memory_space=pltpu.HBM)] * 2,
        out_specs=(in_vmem, in_vmem),
        scratch_shapes=[
            pltpu.VMEM((264 * 16, LANES), f32),
            pltpu.SMEM((8,), jnp.int32),
            pltpu.VMEM((2, 256, 256), jnp.bfloat16),
            pltpu.VMEM((2, 256, 256), jnp.bfloat16),
            pltpu.VMEM((8, 8, 2, CH, LANES), f32),
            window,
            tensor,
            matrix,
            dma((2,)),
            dma((2,)),
            dma((2,)),
            dma((2, 2)),
        ],
        compiler_params=pltpu.CompilerParams(
            collective_id=0, has_side_effects=True, vmem_limit_bytes=40 << 20
        ),
        name="transform_exchange",
    )(x, bins)
    out = pl.pallas_call(
        dips_kernel,
        out_shape=jax.ShapeDtypeStruct((2, 2, 2048, LANES), f32),
        in_specs=[in_vmem, in_vmem],
        out_specs=anywhere,
        scratch_shapes=[tensor, field, matrix, dma((2,))],
        compiler_params=pltpu.CompilerParams(vmem_limit_bytes=32 << 20),
        name="last_band_dips",
    )(dip, last)
    return out.reshape(2, 2, 8, 256, NF)


def solution(mesh):
    in_specs = (P(None, ("band", "tile"), None), P())
    out_specs = P("band", None, "tile", None, None)
    return jax.shard_map(local, mesh=mesh, in_specs=in_specs, out_specs=out_specs, check_vma=False)
```

time: 84.9 us -> 69.9 us (0.82)
  the two profiles are of different devices: /device:TPU:57 before, /device:TPU:1 now
where the time goes in v2:
time: 69.9 us; the launch traced here: 69.8 us
  Pallas kernels  69.8 us (100%)
    pallas_call x1, Pallas kernels, local(): pl.pallas_call(exchange_kernel, out_shape=(jax.ShapeDtypeStruct((2, 2048,...  60.9 us
    pallas_call x1, Pallas kernels, local(): pl.pallas_call(dips_kernel, out_shape=jax.ShapeDtypeStruct((2, 2, 2048, L...  8.88 us

profile of v2, /device:TPU:1, one launch (start us, length us, event | category | flops | bytes accessed | tf_op | source)
XLA Modules:
  0.0 69.8 jit_solution(12892261654108605139)
XLA Ops:
  0.0 60.9 %transform_exchange.1 = (f32[2,2048,128]{2,1,0:T(8,128)S(1)}, f32[4128,128]{1,0:T(8,128)S(1)}) custom-call(f32[4096,128]{1,0:T(8,128)} %bitcast.6, s32[8]{0:T(128)} %bins_hbm.1), custom_call_target="tpu_custom_call" | custom-call | tf_op jit(solution)/shard_map/transform_exchange/pallas_call | solution.py:316
  60.9 8.9 %last_band_dips.1 = f32[2,2,2048,128]{3,2,1,0:T(8,128)} custom-call(f32[2,2048,128]{2,1,0:T(8,128)S(1)} %get-tuple-element.7.dip, f32[4128,128]{1,0:T(8,128)S(1)} %get-tuple-element.8.last), custom_call_target="tpu_custom_call" | custom-call | tf_op jit(solution)/shard_map/last_band_dips/pallas_call | solution.py:343

commit v3 on v2

--- a/solution.py
+++ b/solution.py
@@ -17,13 +17,19 @@
 LANES = 128
 TILES = 4
 CH = 8 * TILES + 8
-GX = 32
+PX = 8
+GX = 64
 
 
 def smooth_weights():
     w = [math.exp(-(k * k) / (2.0 * SIGMA * SIGMA)) for k in range(-R, R + 1)]
     total = sum(w)
     return [v / total for v in w]
+
+
+def side_weights():
+    w = smooth_weights()
+    return [w[R + k] / w[R] for k in range(1, R + 1)]
 
 
 def split(x):
@@ -36,8 +42,9 @@
     frame = lax.broadcasted_iota(jnp.int32, (NF, NF), 1)
     away = jnp.abs(((lane + 4) & (NF - 1)) - frame)
     value = jnp.zeros((NF, NF), jnp.float32)
-    for k, weight in enumerate(smooth_weights()[R:]):
-        value = jnp.where(away == k, weight, value)
+    w = smooth_weights()
+    for k in range(R + 1):
+        value = jnp.where(away == k, w[R + k] * w[R] * w[R], value)
     hi, lo = split(value)
     tmat[pl.ds(0, NF), pl.ds(0, NF)] = hi
     tmat[pl.ds(NF, NF), pl.ds(0, NF)] = hi
@@ -110,38 +117,61 @@
             send[c, b, e] = v[b]
 
 
-def products_step(g, recv, q):
+def products_step(g, recv, taps, slot):
     lane = lax.broadcasted_iota(jnp.int32, (8, LANES), 1)
-    w = smooth_weights()
-
-    def rows(xl, row):
-        return recv[pl.ds((8 * g + xl + 1) * 16 + row, 8, stride=16), :]
-
-    a = [rows(0, r) for r in range(16)]
-    p = [[], [], []]
-    for r in range(1, 15):
-        later = jnp.where(lane == 123, 0.0, pltpu.roll(a[r], LANES - 1, axis=1))
-        earlier = jnp.where(lane == 124, 0.0, pltpu.roll(a[r], 1, axis=1))
-        gt = later - earlier
-        p[0].append((a[r + 1] - a[r - 1]) * gt)
-        p[1].append((rows(1, r) - rows(-1, r)) * gt)
-        p[2].append(gt * gt)
-    for i in range(3):
-        for r in range(8):
-            s = w[3] * p[i][r + 3]
+
+    def rows(xl, first):
+        return recv[pl.ds((PX * g + xl + 1) * 16 + first, 8), :]
+
+    centre = [[rows(x, first) for first in (1, 7)] for x in range(-1, PX + 1)]
+    for x in range(PX):
+        for half, first in enumerate((1, 7)):
+            a = centre[x + 1][half]
+            later = jnp.where(lane == 123, 0.0, pltpu.roll(a, LANES - 1, axis=1))
+            earlier = jnp.where(lane == 124, 0.0, pltpu.roll(a, 1, axis=1))
+            gt = later - earlier
+            gi = rows(x, first + 1) - rows(x, first - 1)
+            gx = centre[x + 2][half] - centre[x][half]
+            for i, p in enumerate((gi * gt, gx * gt, gt * gt)):
+                taps[slot, i, x, pl.ds(first - 1, 8), :] = p
+
+
+def rows_step(g, taps, slot, q):
+    w = side_weights()
+    for x in range(PX):
+        for i in range(3):
+            tap = [taps[slot, i, x, pl.ds(k, 8), :] for k in range(7)]
+            s = tap[3]
             for k in range(1, 4):
-                s = s + w[3 + k] * (p[i][r + 3 - k] + p[i][r + 3 + k])
-            q[i, pl.ds((8 * g + 3) * 8 + r, 8, stride=8), :] = s
-
-
-def smooth_step(g, q, tmat, out):
-    w = smooth_weights()
+                s = s + w[k - 1] * (tap[3 - k] + tap[3 + k])
+            q[i, pl.ds(pl.multiple_of((PX * g + x + 3) * 8, 8), 8), :] = s
+
+
+def tensor_rows(recv, q, taps):
+    last = 256 // PX - 1
+    products_step(0, recv, taps, 0)
+
+    def pair(h, carry):
+        rows_step(2 * h, taps, 0, q)
+        products_step(2 * h + 1, recv, taps, 1)
+        rows_step(2 * h + 1, taps, 1, q)
+        products_step(2 * h + 2, recv, taps, 0)
+        return carry
+
+    lax.fori_loop(0, last // 2, pair, 0)
+    rows_step(last - 1, taps, 0, q)
+    products_step(last, recv, taps, 1)
+    rows_step(last, taps, 1, q)
+
+
+def smooth_step(g, q, tmat, turn, out):
+    w = side_weights()
     sm = []
     for i in range(3):
         load = lambda x: q[i, pl.ds(pl.multiple_of((GX * g + x) * 8, 8), GX * 8), :]
-        s = w[3] * load(3)
+        s = load(3)
         for k in range(1, 4):
-            s = s + w[3 + k] * (load(3 - k) + load(3 + k))
+            s = s + w[k - 1] * (load(3 - k) + load(3 + k))
         sm.append(s)
     hi, lo = split(jnp.concatenate(sm, axis=0))
     t = jnp.dot(
@@ -153,11 +183,21 @@
     for i in range(2):
         d = t[i * m : (i + 1) * m] * inv
         for x in range(GX):
-            out[i, pl.ds(GX * g + x, 8, stride=256), :] = d[8 * x : 8 * x + 8]
+            turn[i, x // 8, pl.ds(x % 8, 8, stride=8), :] = d[8 * x : 8 * x + 8]
+        for block in range(GX // 8):
+            for row in range(8):
+                place = pl.ds(pl.multiple_of(row * 256 + GX * g + 8 * block, 8), 8)
+                out[i, place, :] = turn[i, block, pl.ds(8 * row, 8), :]
+
+
+def clear_rim(q):
+    for i in range(3):
+        for start in (0, 259 * 8):
+            q[i, pl.ds(start, 24), :] = jnp.zeros((24, LANES), jnp.float32)
 
 
 def exchange_kernel(
-    x_hbm, bins_hbm, dip, last, xv, bins_ref, wh, wl, send, recv, q, tmat, in_sem, ssem, rsem, own_sem
+    x_hbm, bins_hbm, dip, last, xv, bins_ref, wh, wl, send, recv, q, tmat, taps, turn, in_sem, ssem, rsem, own_sem
 ):
     band, tile = lax.axis_index("band"), lax.axis_index("tile")
     me = band * 32 + tile
@@ -256,15 +296,11 @@
         copy.wait()
     arrivals(0).wait_recv()
 
-    def prod(g, carry):
-        products_step(g, recv, q)
-        return carry
-
     def smooth(g, carry):
-        smooth_step(g, q, tmat, dip)
-        return carry
-
-    lax.fori_loop(0, 32, prod, 0)
+        smooth_step(g, q, tmat, turn, dip)
+        return carry
+
+    tensor_rows(recv, q, taps)
     lax.fori_loop(0, 256 // GX, smooth, 0)
     for copy in own[2:]:
         copy.wait()
@@ -273,31 +309,40 @@
         arrivals(j).wait_send()
 
 
-def clear_rim(q):
-    for i in range(3):
-        for start in (0, 259 * 8):
-            q[i, pl.ds(start, 24), :] = jnp.zeros((24, LANES), jnp.float32)
-
-
-def dips_kernel(dip, last, out_hbm, q, out, tmat, sems):
+def dips_kernel(dip, last, out_hbm, q, out, tmat, taps, turn, sems, osems):
     give = pltpu.make_async_copy(dip, out_hbm.at[0], sems.at[0])
     give.start()
     clear_rim(q)
     build_time_matrix(tmat)
 
-    def prod(g, carry):
-        products_step(g, last, q)
-        return carry
+    def result(i, g):
+        return [
+            pltpu.make_async_copy(
+                out.at[i, pl.ds(pl.multiple_of(256 * row + GX * g, GX), GX)],
+                out_hbm.at[1, i, pl.ds(pl.multiple_of(256 * row + GX * g, GX), GX)],
+                osems.at[g],
+            )
+            for row in range(8)
+        ]
 
     def smooth(g, carry):
-        smooth_step(g, q, tmat, out)
-        return carry
-
-    lax.fori_loop(0, 32, prod, 0)
+        smooth_step(g, q, tmat, turn, out)
+        for i in range(2):
+            for copy in result(i, g):
+                copy.start()
+        return carry
+
+    tensor_rows(last, q, taps)
     lax.fori_loop(0, 256 // GX, smooth, 0)
-    result = pltpu.make_async_copy(out, out_hbm.at[1], sems.at[1])
-    result.start()
-    result.wait()
+
+    def drain(g, carry):
+        for i in range(2):
+            pltpu.make_async_copy(
+                out.at[i, pl.ds(0, 8 * GX)], out_hbm.at[1, i, pl.ds(0, 8 * GX)], osems.at[g]
+            ).wait()
+        return carry
+
+    lax.fori_loop(0, 256 // GX, drain, 0)
     give.wait()
 
 
@@ -313,6 +358,8 @@
     window = pltpu.VMEM((258 * 16, LANES), f32)
     tensor = pltpu.VMEM((3, 262 * 8, LANES), f32)
     matrix = pltpu.VMEM((2 * NF, 2 * NF), jnp.bfloat16)
+    tap_rows = pltpu.VMEM((2, 3, PX, 16, LANES), f32)
+    turned = pltpu.VMEM((2, GX // 8, 64, LANES), f32)
     dip, last = pl.pallas_call(
         exchange_kernel,
         out_shape=(
@@ -330,6 +377,8 @@
             window,
             tensor,
             matrix,
+            tap_rows,
+            turned,
             dma((2,)),
             dma((2,)),
             dma((2,)),
@@ -345,7 +394,7 @@
         out_shape=jax.ShapeDtypeStruct((2, 2, 2048, LANES), f32),
         in_specs=[in_vmem, in_vmem],
         out_specs=anywhere,
-        scratch_shapes=[tensor, field, matrix, dma((2,))],
+        scratch_shapes=[tensor, field, matrix, tap_rows, turned, dma((2,)), dma((8,))],
         compiler_params=pltpu.CompilerParams(vmem_limit_bytes=32 << 20),
         name="last_band_dips",
     )(dip, last)

time: 69.9 us -> 67.1 us (0.960)
  Pallas kernels: 69.8 us -> 67 us
    pallas_call x1, Pallas kernels: 8.88 us -> 6.1 us  [local(): pl.pallas_call(dips_kernel, out_shape=jax.ShapeDtypeStruct((2, 2, 2048, L...]
where the time goes in v3:
time: 67.1 us; the launch traced here: 67 us
  Pallas kernels  67 us (100%)
    pallas_call x1, Pallas kernels, local(): pl.pallas_call(exchange_kernel, out_shape=(jax.ShapeDtypeStruct((2, 2048,...  60.9 us
    pallas_call x1, Pallas kernels, local(): pl.pallas_call(dips_kernel, out_shape=jax.ShapeDtypeStruct((2, 2, 2048, L...  6.1 us

profile of v3, /device:TPU:1, one launch (start us, length us, event | category | flops | bytes accessed | tf_op | source)
XLA Modules:
  0.0 67.0 jit_solution(4815370698768792248)
XLA Ops:
  0.0 60.9 %transform_exchange.1 = (f32[2,2048,128]{2,1,0:T(8,128)S(1)}, f32[4128,128]{1,0:T(8,128)S(1)}) custom-call(f32[4096,128]{1,0:T(8,128)} %bitcast.6, s32[8]{0:T(128)} %bins_hbm.1), custom_call_target="tpu_custom_call" | custom-call | tf_op jit(solution)/shard_map/transform_exchange/pallas_call | solution.py:363
  60.9 6.1 %last_band_dips.1 = f32[2,2,2048,128]{3,2,1,0:T(8,128)} custom-call(f32[2,2048,128]{2,1,0:T(8,128)S(1)} %get-tuple-element.7.dip, f32[4128,128]{1,0:T(8,128)S(1)} %get-tuple-element.8.last), custom_call_target="tpu_custom_call" | custom-call | tf_op jit(solution)/shard_map/last_band_dips/pallas_call | solution.py:392

commit v4 on v3

--- a/solution.py
+++ b/solution.py
@@ -287,7 +287,7 @@
         )
 
     def second(k, carry):
-        push(1, (k * 75) & 127)
+        push(1, (k * 83) & 127)
         return carry
 
     lax.fori_loop(1, 128, second, 0)

time: 67.1 us -> 66.7 us (level)
  no operation moved by 1% of the time
where the time goes in v4:
time: 66.7 us; the launch traced here: 66.6 us
  Pallas kernels  66.6 us (100%)
    pallas_call x1, Pallas kernels, local(): pl.pallas_call(exchange_kernel, out_shape=(jax.ShapeDtypeStruct((2, 2048,...  60.5 us
    pallas_call x1, Pallas kernels, local(): pl.pallas_call(dips_kernel, out_shape=jax.ShapeDtypeStruct((2, 2, 2048, L...  6.1 us

profile of v4, /device:TPU:1, one launch (start us, length us, event | category | flops | bytes accessed | tf_op | source)
XLA Modules:
  0.0 66.6 jit_solution(3596683981476575755)
XLA Ops:
  0.0 60.5 %transform_exchange.1 = (f32[2,2048,128]{2,1,0:T(8,128)S(1)}, f32[4128,128]{1,0:T(8,128)S(1)}) custom-call(f32[4096,128]{1,0:T(8,128)} %bitcast.6, s32[8]{0:T(128)} %bins_hbm.1), custom_call_target="tpu_custom_call" | custom-call | tf_op jit(solution)/shard_map/transform_exchange/pallas_call | solution.py:363
  60.5 6.1 %last_band_dips.1 = f32[2,2,2048,128]{3,2,1,0:T(8,128)} custom-call(f32[2,2048,128]{2,1,0:T(8,128)S(1)} %get-tuple-element.7.dip, f32[4128,128]{1,0:T(8,128)S(1)} %get-tuple-element.8.last), custom_call_target="tpu_custom_call" | custom-call | tf_op jit(solution)/shard_map/last_band_dips/pallas_call | solution.py:392

commit v5 on v4

--- a/solution.py
+++ b/solution.py
@@ -287,7 +287,7 @@
         )
 
     def second(k, carry):
-        push(1, (k * 83) & 127)
+        push(1, (k * 115) & 127)
         return carry
 
     lax.fori_loop(1, 128, second, 0)

time: 66.7 us -> 67.1 us (level)
  no operation moved by 1% of the time
where the time goes in v5:
time: 67.1 us; the launch traced here: 67 us
  Pallas kernels  67 us (100%)
    pallas_call x1, Pallas kernels, local(): pl.pallas_call(exchange_kernel, out_shape=(jax.ShapeDtypeStruct((2, 2048,...  60.9 us
    pallas_call x1, Pallas kernels, local(): pl.pallas_call(dips_kernel, out_shape=jax.ShapeDtypeStruct((2, 2, 2048, L...  6.1 us

profile of v5, /device:TPU:1, one launch (start us, length us, event | category | flops | bytes accessed | tf_op | source)
XLA Modules:
  0.0 67.0 jit_solution(3978597798843495391)
XLA Ops:
  0.0 60.9 %transform_exchange.1 = (f32[2,2048,128]{2,1,0:T(8,128)S(1)}, f32[4128,128]{1,0:T(8,128)S(1)}) custom-call(f32[4096,128]{1,0:T(8,128)} %bitcast.6, s32[8]{0:T(128)} %bins_hbm.1), custom_call_target="tpu_custom_call" | custom-call | tf_op jit(solution)/shard_map/transform_exchange/pallas_call | solution.py:363
  60.9 6.1 %last_band_dips.1 = f32[2,2,2048,128]{3,2,1,0:T(8,128)} custom-call(f32[2,2048,128]{2,1,0:T(8,128)S(1)} %get-tuple-element.7.dip, f32[4128,128]{1,0:T(8,128)S(1)} %get-tuple-element.8.last), custom_call_target="tpu_custom_call" | custom-call | tf_op jit(solution)/shard_map/last_band_dips/pallas_call | solution.py:392
